TPU v7x, 32 devices: a whole 2x2x4 slice. The times are simulated.
32 devices in a mesh: dp: 4 (over x, core), fsdp: 8 (over z, y).
Axes of the slice: x: 2, y: 2, z: 4, core: 2. Of those that a mesh axis runs over, the one named last changes fastest.
Arguments:
- tokens: bfloat16 [2, 4096, 1024], P(None, ('dp', 'fsdp')), may hold values from -6 to 6
- scene_ids: int32 [2, 4, 1024], P(None, 'dp', 'fsdp'), may hold values from 0 to 1, never falling along the last dimension, each value on 1 to 682 neighbouring positions
- w_qkv: bfloat16 [1024, 3072], P(('dp', 'fsdp')), may hold values from -0.1875 to 0.1875
- w_out: bfloat16 [1024, 1024], P(('dp', 'fsdp')), may hold values from -6 to 6
- w_up: bfloat16 [1024, 4096], P(('dp', 'fsdp')), may hold values from -0.1875 to 0.1875
- w_down: bfloat16 [4096, 1024], P(('dp', 'fsdp')), may hold values from -0.09375 to 0.09375
- gain_one: bfloat16 [1024], P(('dp', 'fsdp')), may hold values from 0.5 to 1.5
- bias_one: bfloat16 [1024], P(('dp', 'fsdp')), may hold values from -1 to 1
- gain_two: bfloat16 [1024], P(('dp', 'fsdp')), may hold values from 0.5 to 1.5
- bias_two: bfloat16 [1024], P(('dp', 'fsdp')), may hold values from -1 to 1
- cotangent: bfloat16 [2, 4096, 1024], P(None, ('dp', 'fsdp')), may hold values from -6 to 6
Outputs:
- output: bfloat16 [2, 4096, 1024], P(None, ('dp', 'fsdp'))
- input_grad: float32 [2, 4096, 1024], P(None, ('dp', 'fsdp'))
- grad_qkv: float32 [1024, 3072], P(('dp', 'fsdp'))
- grad_out: float32 [1024, 1024], P(('dp', 'fsdp'))
- grad_up: float32 [1024, 4096], P(('dp', 'fsdp'))
- grad_down: float32 [4096, 1024], P(('dp', 'fsdp'))
- grad_gain_one: float32 [1024], P(('dp', 'fsdp'))
- grad_bias_one: float32 [1024], P(('dp', 'fsdp'))
- grad_gain_two: float32 [1024], P(('dp', 'fsdp'))
- grad_bias_two: float32 [1024], P(('dp', 'fsdp'))
Inputs may be any that keep to these rules, and one draw needn't show every extreme that they name: `scene_ids`: in each scene group of a micro-batch the scene numbers never fall, each of the 2 scenes holds 1 to 682 tokens.
All inputs are finite; a program needn't handle non-finite values.
Results may differ from a plain program's by a relative error of at most 0.012.
Values may be sent and summed in bfloat16 or wider, within the bound.
No kernel may reach another device: no remote copies, remote signals or barrier semaphores. Data moves between devices by JAX's collectives and lax.ppermute only.
A program may use at most 320 MiB of HBM per device.

v0:
```python
import math
import jax
import jax.numpy as jnp
from jax import lax
from jax.sharding import PartitionSpec as P

HEAD_DIM = 64
eps_norm = 1e-05
lowest_score = -1000000000.0


def layer_norm(values, gain, shift):
    average = jnp.mean(values, axis=-1, keepdims=True)
    centered = values - average
    variance = jnp.mean(centered * centered, axis=-1, keepdims=True)
    return centered * lax.rsqrt(variance + eps_norm) * gain + shift


def exact_gelu(values):
    return jax.nn.gelu(values, approximate=False)


def key_blocks(kv_all, key_scene):
    total = kv_all.shape[0]
    size = 512
    return (
        kv_all.reshape(total // size, size, kv_all.shape[1]),
        key_scene.reshape(total // size, size),
    )


def block_scores(queries, block, scenes, own_scene):
    scale = 1.0 / math.sqrt(HEAD_DIM)
    width = block.shape[1] // 2
    key_heads = block[:, :width].reshape(block.shape[0], -1, HEAD_DIM)
    scores = (
        jnp.einsum("qhd,khd->hqk", queries, key_heads, preferred_element_type=jnp.float32) * scale
    )
    same_scene = own_scene[:, None] == scenes[None, :]
    return jnp.where(same_scene[None], scores, lowest_score)


def block_values(block):
    width = block.shape[1] // 2
    return block[:, width:].reshape(block.shape[0], -1, HEAD_DIM)


def attention_forward(query_cols, kv_all, own_scene, key_scene):
    row_count = query_cols.shape[0]
    queries = query_cols.reshape(row_count, -1, HEAD_DIM)
    head_count = queries.shape[1]
    blocks, scenes = key_blocks(kv_all, key_scene)

    def peak_step(carry, item):
        peak, total = carry
        masked = block_scores(queries, item[0], item[1], own_scene)
        new_peak = jnp.maximum(peak, jnp.max(masked, axis=-1, keepdims=True))
        total = total * jnp.exp(peak - new_peak) + jnp.sum(
            jnp.exp(masked - new_peak), axis=-1, keepdims=True
        )
        return ((new_peak, total), None)

    start = (
        jnp.full((head_count, row_count, 1), -jnp.inf, jnp.float32),
        jnp.zeros((head_count, row_count, 1), jnp.float32),
    )
    (peak, total), unused = lax.scan(peak_step, start, (blocks, scenes))
    log_total = peak + jnp.log(total)

    def mix_step(accum, item):
        masked = block_scores(queries, item[0], item[1], own_scene)
        probs = jnp.exp(masked - log_total).astype(jnp.bfloat16)
        return (
            accum
            + jnp.einsum(
                "hqk,khd->qhd", probs, block_values(item[0]), preferred_element_type=jnp.float32
            ),
            None,
        )

    mixed, unused = lax.scan(
        mix_step, jnp.zeros((row_count, head_count, HEAD_DIM), jnp.float32), (blocks, scenes)
    )
    return (mixed.reshape(row_count, -1).astype(jnp.bfloat16), log_total)


def attention_backward(query_cols, kv_all, own_scene, key_scene, log_total, grad_mixed):
    scale = 1.0 / math.sqrt(HEAD_DIM)
    row_count = query_cols.shape[0]
    queries = query_cols.reshape(row_count, -1, HEAD_DIM)
    head_count = queries.shape[1]
    grad_heads = grad_mixed.reshape(row_count, -1, HEAD_DIM)
    blocks, scenes = key_blocks(kv_all, key_scene)

    def inner_step(inner, item):
        masked = block_scores(queries, item[0], item[1], own_scene)
        probs = jnp.exp(masked - log_total)
        grad_probs = jnp.einsum(
            "qhd,khd->hqk", grad_heads, block_values(item[0]), preferred_element_type=jnp.float32
        )
        return (inner + jnp.sum(probs * grad_probs, axis=-1, keepdims=True), None)

    inner, unused = lax.scan(
        inner_step, jnp.zeros((head_count, row_count, 1), jnp.float32), (blocks, scenes)
    )

    def grad_step(grad_queries, item):
        block = item[0]
        width = block.shape[1] // 2
        key_heads = block[:, :width].reshape(block.shape[0], -1, HEAD_DIM)
        masked = block_scores(queries, block, item[1], own_scene)
        probs = jnp.exp(masked - log_total)
        grad_probs = jnp.einsum(
            "qhd,khd->hqk", grad_heads, block_values(block), preferred_element_type=jnp.float32
        )
        grad_scores = (probs * (grad_probs - inner)).astype(jnp.bfloat16)
        grad_queries = (
            grad_queries
            + jnp.einsum("hqk,khd->qhd", grad_scores, key_heads, preferred_element_type=jnp.float32)
            * scale
        )
        grad_keys = (
            jnp.einsum("hqk,qhd->khd", grad_scores, queries, preferred_element_type=jnp.float32)
            * scale
        )
        grad_values = jnp.einsum(
            "hqk,qhd->khd",
            probs.astype(jnp.bfloat16),
            grad_heads,
            preferred_element_type=jnp.float32,
        )
        both = jnp.concatenate(
            [grad_keys.reshape(block.shape[0], -1), grad_values.reshape(block.shape[0], -1)], axis=1
        )
        return (grad_queries, both)

    grad_queries, grad_pairs = lax.scan(
        grad_step, jnp.zeros((row_count, head_count, HEAD_DIM), jnp.float32), (blocks, scenes)
    )
    return (grad_queries.reshape(row_count, -1), grad_pairs.reshape(kv_all.shape[0], -1))


def outer_sum(left, right):
    return jnp.einsum("ti,tj->ij", left, right, preferred_element_type=jnp.float32)


def back_product(grad_rows, weight):
    return jnp.einsum("tj,ij->ti", grad_rows, weight, preferred_element_type=jnp.float32)


def body(
    tokens, scene_ids, w_qkv, w_out, w_up, w_down, gain_one, bias_one, gain_two, bias_two, cotangent
):
    micro_count = tokens.shape[0]
    all_scenes = lax.all_gather(scene_ids, "fsdp", axis=2, tiled=True)
    totals = (
        jnp.zeros(w_qkv.shape, jnp.float32),
        jnp.zeros(w_out.shape, jnp.float32),
        jnp.zeros(w_up.shape, jnp.float32),
        jnp.zeros(w_down.shape, jnp.float32),
        jnp.zeros(gain_one.shape, jnp.float32),
        jnp.zeros(bias_one.shape, jnp.float32),
        jnp.zeros(gain_two.shape, jnp.float32),
        jnp.zeros(bias_two.shape, jnp.float32),
    )
    results = []
    input_grads = []
    for batch_index in range(micro_count):
        forward_weights = (
            lax.all_gather(w_qkv, ("dp", "fsdp"), axis=0, tiled=True),
            lax.all_gather(w_out, ("dp", "fsdp"), axis=0, tiled=True),
            lax.all_gather(w_up, ("dp", "fsdp"), axis=0, tiled=True),
            lax.all_gather(w_down, ("dp", "fsdp"), axis=0, tiled=True),
            lax.all_gather(gain_one, ("dp", "fsdp"), axis=0, tiled=True),
            lax.all_gather(bias_one, ("dp", "fsdp"), axis=0, tiled=True),
            lax.all_gather(gain_two, ("dp", "fsdp"), axis=0, tiled=True),
            lax.all_gather(bias_two, ("dp", "fsdp"), axis=0, tiled=True),
        )
        full_qkv, full_out, full_up, full_down, full_gone, full_bone, full_gtwo, full_btwo = (
            forward_weights
        )
        width = full_qkv.shape[1] // 3
        block_tokens = tokens[batch_index].astype(jnp.float32)
        own_scene = scene_ids[batch_index, 0]
        key_scene = all_scenes[batch_index, 0]
        normed_one, pull_one = jax.vjp(
            layer_norm, block_tokens, full_gone.astype(jnp.float32), full_bone.astype(jnp.float32)
        )
        normed_one_low = normed_one.astype(jnp.bfloat16)
        projected = jnp.dot(normed_one_low, full_qkv, preferred_element_type=jnp.float32).astype(
            jnp.bfloat16
        )
        query_cols = projected[:, :width]
        kv_all = lax.all_gather(projected[:, width:], "fsdp", axis=0, tiled=True)
        mixed_low, log_total = attention_forward(query_cols, kv_all, own_scene, key_scene)
        hidden = block_tokens + jnp.dot(mixed_low, full_out, preferred_element_type=jnp.float32)
        normed_two, pull_two = jax.vjp(
            layer_norm, hidden, full_gtwo.astype(jnp.float32), full_btwo.astype(jnp.float32)
        )
        normed_two_low = normed_two.astype(jnp.bfloat16)
        upward = jnp.dot(normed_two_low, full_up, preferred_element_type=jnp.float32)
        activated, pull_gelu = jax.vjp(exact_gelu, upward)
        activated_low = activated.astype(jnp.bfloat16)
        result = hidden + jnp.dot(activated_low, full_down, preferred_element_type=jnp.float32)
        results.append(result.astype(jnp.bfloat16))
        backward_weights = (
            lax.all_gather(w_qkv, ("dp", "fsdp"), axis=0, tiled=True),
            lax.all_gather(w_out, ("dp", "fsdp"), axis=0, tiled=True),
            lax.all_gather(w_up, ("dp", "fsdp"), axis=0, tiled=True),
            lax.all_gather(w_down, ("dp", "fsdp"), axis=0, tiled=True),
            lax.all_gather(gain_one, ("dp", "fsdp"), axis=0, tiled=True),
            lax.all_gather(bias_one, ("dp", "fsdp"), axis=0, tiled=True),
            lax.all_gather(gain_two, ("dp", "fsdp"), axis=0, tiled=True),
            lax.all_gather(bias_two, ("dp", "fsdp"), axis=0, tiled=True),
        )
        back_qkv, back_out, back_up, back_down = (
            backward_weights[0],
            backward_weights[1],
            backward_weights[2],
            backward_weights[3],
        )
        grad_result = cotangent[batch_index].astype(jnp.float32)
        grad_result_low = grad_result.astype(jnp.bfloat16)
        local_down = outer_sum(activated_low, grad_result_low)
        grad_act = back_product(grad_result_low, back_down)
        grad_upward = pull_gelu(grad_act)[0].astype(jnp.bfloat16)
        local_up = outer_sum(normed_two_low, grad_upward)
        grad_norm_two = back_product(grad_upward, back_up)
        grad_hidden_part, local_gtwo, local_btwo = pull_two(grad_norm_two)
        grad_hidden = grad_result + grad_hidden_part
        grad_hidden_low = grad_hidden.astype(jnp.bfloat16)
        local_out = outer_sum(mixed_low, grad_hidden_low)
        grad_mixed = back_product(grad_hidden_low, back_out).astype(jnp.bfloat16)
        grad_queries, grad_pairs = attention_backward(
            query_cols, kv_all, own_scene, key_scene, log_total, grad_mixed
        )
        grad_own_pairs = lax.psum_scatter(
            grad_pairs.astype(jnp.bfloat16), "fsdp", scatter_dimension=0, tiled=True
        ).astype(jnp.float32)
        grad_projected = jnp.concatenate([grad_queries, grad_own_pairs], axis=1).astype(
            jnp.bfloat16
        )
        local_qkv = outer_sum(normed_one_low, grad_projected)
        grad_norm_one = back_product(grad_projected, back_qkv)
        grad_token_part, local_gone, local_bone = pull_one(grad_norm_one)
        input_grads.append(grad_hidden + grad_token_part)
        summed = (
            lax.psum_scatter(local_qkv, ("dp", "fsdp"), scatter_dimension=0, tiled=True),
            lax.psum_scatter(local_out, ("dp", "fsdp"), scatter_dimension=0, tiled=True),
            lax.psum_scatter(local_up, ("dp", "fsdp"), scatter_dimension=0, tiled=True),
            lax.psum_scatter(local_down, ("dp", "fsdp"), scatter_dimension=0, tiled=True),
            lax.psum_scatter(local_gone, ("dp", "fsdp"), scatter_dimension=0, tiled=True),
            lax.psum_scatter(local_bone, ("dp", "fsdp"), scatter_dimension=0, tiled=True),
            lax.psum_scatter(local_gtwo, ("dp", "fsdp"), scatter_dimension=0, tiled=True),
            lax.psum_scatter(local_btwo, ("dp", "fsdp"), scatter_dimension=0, tiled=True),
        )
        totals = jax.tree.map(jnp.add, totals, tuple(summed))
    output = jnp.stack(results, axis=0)
    input_grad = jnp.stack(input_grads, axis=0)
    return (
        output,
        input_grad,
        totals[0],
        totals[1],
        totals[2],
        totals[3],
        totals[4],
        totals[5],
        totals[6],
        totals[7],
    )


def solution(mesh):
    return jax.shard_map(
        body,
        mesh=mesh,
        in_specs=(
            P(None, ("dp", "fsdp"), None),
            P(None, "dp", "fsdp"),
            P(("dp", "fsdp"), None),
            P(("dp", "fsdp"), None),
            P(("dp", "fsdp"), None),
            P(("dp", "fsdp"), None),
            P(("dp", "fsdp")),
            P(("dp", "fsdp")),
            P(("dp", "fsdp")),
            P(("dp", "fsdp")),
            P(None, ("dp", "fsdp"), None),
        ),
        out_specs=(
            P(None, ("dp", "fsdp"), None),
            P(None, ("dp", "fsdp"), None),
            P(("dp", "fsdp"), None),
            P(("dp", "fsdp"), None),
            P(("dp", "fsdp"), None),
            P(("dp", "fsdp"), None),
            P(("dp", "fsdp")),
            P(("dp", "fsdp")),
            P(("dp", "fsdp")),
            P(("dp", "fsdp")),
        ),
        check_vma=False,
    )
```

profile of v0, /device:TPU:0, one launch (start us, length us, event | category | flops | bytes accessed | tf_op | source)
XLA Modules:
  0.0 1742.1 jit_solution(13039055786084457197)
XLA Ops:
  11.3 42.4 %all-reduce.9 = (bf16[1024]{0:T(1024)(128)(2,1)S(1)}, bf16[1024]{0:T(1024)(128)(2,1)S(1)}, bf16[1024]{0:T(1024)(128)(2,1)S(1)}, bf16[1024]{0:T(1024)(128)(2,1)S(1)}) all-reduce(bf16[1024]{0:T(1024)(128)(2,1)S(1)} %dynamic-update-slice.1, bf16[1024]{0:T(1024)(128)(2,1)S(1)} %dynamic-update-slice, ...), channel_id=1, replica_groups=mesh['dp'=4,'fsdp'=8] {'dp','fsdp'}, use_global_device_ids=true, to_apply=%add.1 | all-reduce | flops 4096 | bytes 16384
  56.3 26.9 %all-gather.7.cloned.1.call-done = bf16[1024,3072]{1,0:T(8,128)(2,1)} async-done(((bf16[32,3072]{1,0:T(8,128)(2,1)}), bf16[1024,3072]{1,0:T(8,128)(2,1)}) %all-gather.7.cloned.1.call-update) | async-done | bytes 6291472 | tf_op jit(solution)/shard_map/all_gather | solution.py:170
  94.9 19.6 %all_gather.26 = s32[2,1,1024]{2,1,0:T(1,128)S(1)} all-gather(s32[2,1,128]{2,1,0:T(1,128)S(1)} %copy-done.82), channel_id=1, replica_groups=mesh['dp'=4,'fsdp'=8] {'fsdp'}, dimensions={2}, use_global_device_ids=true | all-gather | bytes 9216 | tf_op jit(solution)/shard_map/all_gather | solution.py:155
  115.0 45.2 %all-gather.17.cloned.1.call-done = bf16[1024,2048]{1,0:T(8,128)(2,1)} async-done(((bf16[128,2048]{1,0:T(8,128)(2,1)}), bf16[1024,2048]{1,0:T(8,128)(2,1)}) %all-gather.17.cloned.1.call-update) | async-done | bytes 4194320 | tf_op jit(solution)/shard_map/all_gather | solution.py:194
  166.5 15.9 while.98
  182.4 10.1 while.99
  193.7 40.9 %all-gather.9.cloned.1.call-done = bf16[1024,2048]{1,0:T(8,128)(2,1)} async-done(((bf16[128,2048]{1,0:T(8,128)(2,1)}), bf16[1024,2048]{1,0:T(8,128)(2,1)}) %all-gather.9.cloned.1.call-update) | async-done | bytes 4194320 | tf_op jit(solution)/shard_map/all_gather | solution.py:194
  240.8 16.0 while.96
  256.9 10.2 while.97
  268.2 24.1 %all-gather.11.cloned.1.call-done = bf16[1024,1024]{1,0:T(8,128)(2,1)} async-done(((bf16[32,1024]{1,0:T(8,128)(2,1)}), bf16[1024,1024]{1,0:T(8,128)(2,1)}) %all-gather.11.cloned.1.call-update) | async-done | bytes 2097168 | tf_op jit(solution)/shard_map/all_gather | solution.py:171
  295.6 75.8 %all-gather.13.cloned.1.call-done = bf16[1024,4096]{1,0:T(8,128)(2,1)} async-done(((bf16[32,4096]{1,0:T(8,128)(2,1)}), bf16[1024,4096]{1,0:T(8,128)(2,1)}) %all-gather.13.cloned.1.call-update) | async-done | bytes 8388624 | tf_op jit(solution)/shard_map/all_gather | solution.py:172
  380.3 69.9 %all-gather.15.cloned.1.call-done = bf16[4096,1024]{1,0:T(8,128)(2,1)} async-done(((bf16[128,1024]{1,0:T(8,128)(2,1)}), bf16[4096,1024]{1,0:T(8,128)(2,1)}) %all-gather.15.cloned.1.call-update) | async-done | bytes 8388624 | tf_op jit(solution)/shard_map/all_gather | solution.py:173
  450.3 10.1 add_convert_fusion
  467.2 7.6 add_convert_fusion.1
  483.3 8.9 while.100
  494.7 34.5 %while.101 = (s32[]{:T(128)}, f32[128,16,64]{0,2,1:T(8,128)}, bf16[2,512,2048]{2,1,0:T(8,128)(2,1)}, bf16[2,512,2048]{1,2,0:T(8,128)(2,1)}, s32[1,1,128]{2,1,0:T...) while((s32[]{:T(128)}, f32[128,16,64]{0,2,1:T(8,128)}, ...), condition=%wide.region_26.27_spmd.clone, body=%wide.region_25.26_spmd.clone.sunk | while | flops 687276032 | bytes 83065600 | solution.py:137
  530.2 11.2 while.102
  543.9 34.3 %while.103 = (s32[]{:T(128)}, f32[128,16,64]{0,2,1:T(8,128)}, bf16[2,512,2048]{2,1,0:T(8,128)(2,1)}, bf16[2,512,2048]{1,2,0:T(8,128)(2,1)}, s32[1,1,128]{2,1,0:T...) while((s32[]{:T(128)}, f32[128,16,64]{0,2,1:T(8,128)}, ...), condition=%wide.region_36.37_spmd.clone, body=%wide.region_35.36_spmd.clone.sunk | while | flops 687276032 | bytes 80968392 | solution.py:137
  584.2 31.9 %reduce-scatter.7.cloned.1.call-done = bf16[128,2048]{1,0:T(8,128)(2,1)} async-done(((bf16[1024,2048]{1,0:T(8,128)(2,1)}), bf16[128,2048]{1,0:T(8,128)(2,1)}) %reduce-scatter.7.cloned.1.call-update) | async-done | bytes 524304 | tf_op jit(solution)/shard_map/reduce_scatter | solution.py:237
  616.1 7.5 fusion.95
  623.6 84.4 %reduce-scatter.9.cloned.1.call-done = bf16[128,2048]{1,0:T(8,128)(2,1)} async-done(((bf16[1024,2048]{1,0:T(8,128)(2,1)}), bf16[128,2048]{1,0:T(8,128)(2,1)}) %reduce-scatter.9.cloned.1.call-update) | async-done | bytes 524304 | tf_op jit(solution)/shard_map/reduce_scatter | solution.py:237
  708.0 11.2 convolution_add_fusion.2
  724.0 8.3 convolution_add_fusion.1
  733.3 11.1 fusion.104
  744.4 13.3 convolution_add_fusion
  758.5 9.6 fusion.68
  768.1 8.3 fusion.69
  782.5 42.9 %all-reduce.8 = (f32[1024]{0:T(1024)S(1)}, f32[1024]{0:T(1024)S(1)}, f32[1024]{0:T(1024)S(1)}, f32[1024]{0:T(1024)S(1)}) all-reduce(f32[1024]{0:T(1024)S(1)} %add.238, f32[1024]{0:T(1024)S(1)} %add.239, f32[1024]{0:T(1024)S(1)} %add.240, f32[1024]{0:T(1024)S(1)} %add.241), channel_id=16, replica_groups=mesh['dp'=4,'fsdp'=8] {'dp','fsdp'}, use_global_device_ids=true, to_apply=%region_49.50.clone | all-reduce | flops 4096 | bytes 32768
  829.3 25.3 %reduce-scatter.13.cloned.1.call-done = f32[32,1024]{1,0:T(8,128)} async-done(((f32[1024,1024]{1,0:T(8,128)}), f32[32,1024]{1,0:T(8,128)}) %reduce-scatter.13.cloned.1.call-update) | async-done | bytes 131088 | tf_op jit(solution)/shard_map/reduce_scatter | solution.py:249
  854.6 160.0 %reduce-scatter.11.cloned.1.call-done = f32[32,3072]{1,0:T(8,128)} async-done(((f32[1024,3072]{1,0:T(8,128)}), f32[32,3072]{1,0:T(8,128)}) %reduce-scatter.11.cloned.1.call-update) | async-done | bytes 393232 | tf_op jit(solution)/shard_map/reduce_scatter | solution.py:248
  1014.6 360.2 %reduce-scatter.15.cloned.1.call-done = f32[32,4096]{1,0:T(8,128)} async-done(((f32[1024,4096]{1,0:T(8,128)}), f32[32,4096]{1,0:T(8,128)}) %reduce-scatter.15.cloned.1.call-update) | async-done | bytes 524304 | tf_op jit(solution)/shard_map/reduce_scatter | solution.py:250
  1374.8 360.2 %reduce-scatter.17.cloned.1.call-done = f32[128,1024]{1,0:T(8,128)} async-done(((f32[4096,1024]{1,0:T(8,128)}), f32[128,1024]{1,0:T(8,128)}) %reduce-scatter.17.cloned.1.call-update) | async-done | bytes 524304 | tf_op jit(solution)/shard_map/reduce_scatter | solution.py:251
  (456 shorter events, 228.1 us)
Async XLA Ops:
  7.2 76.1 %all-gather.7.cloned.1.call-start = ((), (), s32[]{:S(2)}) async-start(), calls=%async_computation.6 | async-start | bytes 6488064 | tf_op jit(solution)/shard_map/all_gather | solution.py:170
  7.9 152.3 %all-gather.17.cloned.1.call-start = ((), (), s32[]{:S(2)}) async-start(), calls=%async_computation.11 | async-start | bytes 4718592 | tf_op jit(solution)/shard_map/all_gather | solution.py:194
  88.1 146.5 %all-gather.9.cloned.1.call-start = ((), (), s32[]{:S(2)}) async-start(), calls=%async_computation.7 | async-start | bytes 4718592 | tf_op jit(solution)/shard_map/all_gather | solution.py:194
  93.0 199.3 %all-gather.11.cloned.1.call-start = ((), (), s32[]{:S(2)}) async-start(), calls=%async_computation.8 | async-start | bytes 2162688 | tf_op jit(solution)/shard_map/all_gather | solution.py:171
  93.5 277.9 %all-gather.13.cloned.1.call-start = ((), (), s32[]{:S(2)}) async-start(), calls=%async_computation.9 | async-start | bytes 8650752 | tf_op jit(solution)/shard_map/all_gather | solution.py:172
  94.1 356.1 %all-gather.15.cloned.1.call-start = ((), (), s32[]{:S(2)}) async-start(), calls=%async_computation.10 | async-start | bytes 8650752 | tf_op jit(solution)/shard_map/all_gather | solution.py:173
  94.7 521.4 %reduce-scatter.7.cloned.1.call-start = ((), (), s32[]{:S(2)}) async-start(), calls=%async_computation.12 | async-start | bytes 4718592 | tf_op jit(solution)/shard_map/reduce_scatter | solution.py:237
  114.5 263.1 %copy-start.45 = (f32[1024]{0:T(1024)}, f32[1024]{0:T(1024)S(1)}, u32[]{:S(2)}) copy-start(f32[1024]{0:T(1024)S(1)} %convert_element_type.139) | copy-start | bytes 12292
  114.6 363.9 %copy-start.41 = (f32[1024]{0:T(1024)}, f32[1024]{0:T(1024)S(1)}, u32[]{:S(2)}) copy-start(f32[1024]{0:T(1024)S(1)} %convert_element_type.138) | copy-start | bytes 12292
  192.5 48.3 %copy-start.1 = (bf16[128,16,64]{0,2,1:T(8,128)(2,1)}, bf16[128,16,64]{0,2,1:T(8,128)(2,1)S(1)}, u32[]{:S(2)}) copy-start(bf16[128,16,64]{0,2,1:T(8,128)(2,1)S(1)} %get-tuple-element.1718) | copy-start | bytes 786436
  192.5 48.3 %copy-start.50 = (s32[2,512]{1,0:T(2,128)}, s32[2,512]{1,0:T(2,128)S(1)}, u32[]{:S(2)}) copy-start(s32[2,512]{1,0:T(2,128)S(1)} %get-tuple-element.1743) | copy-start | bytes 12292
  192.5 48.3 %copy-start.54 = (s32[1,1,128]{2,1,0:T(1,128)}, s32[1,1,128]{2,1,0:T(1,128)S(1)}, u32[]{:S(2)}) copy-start(s32[1,1,128]{2,1,0:T(1,128)S(1)} %get-tuple-element.1754) | copy-start | bytes 1540
  192.5 48.3 %copy-start.80 = (f32[16,128,1]{1,0,2:T(8,128)}, f32[16,128,1]{1,0,2:T(8,128)S(1)}, u32[]{:S(2)}) copy-start(f32[16,128,1]{1,0,2:T(8,128)S(1)} %get-tuple-element.1763) | copy-start | bytes 24580
  193.7 98.6 %copy-start.24 = (bf16[128,16,64]{0,2,1:T(8,128)(2,1)}, bf16[128,16,64]{0,2,1:T(8,128)(2,1)S(1)}, u32[]{:S(2)}) copy-start(bf16[128,16,64]{0,2,1:T(8,128)(2,1)S(1)} %convert_element_type.147) | copy-start | bytes 786436
  294.6 183.9 %copy-start.11 = (f32[128,1024]{1,0:T(8,128)}, f32[128,1024]{1,0:T(8,128)S(1)}, u32[]{:S(2)}) copy-start(f32[128,1024]{1,0:T(8,128)S(1)} %get-tuple-element.1024) | copy-start | bytes 1572868
  294.6 183.9 %copy-start.63 = (f32[128]{0:T(128)}, f32[128]{0:T(128)S(1)}, u32[]{:S(2)}) copy-start(f32[128]{0:T(128)S(1)} %broadcast_multiply_fusion) | copy-start | bytes 1540
  295.4 183.1 %copy-start.13 = (f32[128,1024]{1,0:T(8,128)}, f32[128,1024]{1,0:T(8,128)S(1)}, u32[]{:S(2)}) copy-start(f32[128,1024]{1,0:T(8,128)S(1)} %get-tuple-element.1026) | copy-start | bytes 1572868
  295.4 183.1 %copy-start.65 = (f32[128]{0:T(128)}, f32[128]{0:T(128)S(1)}, u32[]{:S(2)}) copy-start(f32[128]{0:T(128)S(1)} %broadcast_multiply_fusion.2) | copy-start | bytes 1540
  295.6 182.9 %copy-start.72 = (f32[128]{0:T(128)}, f32[128]{0:T(128)S(1)}, u32[]{:S(2)}) copy-start(f32[128]{0:T(128)S(1)} %fusion.117) | copy-start | bytes 1540
  295.6 182.9 %copy-start.74 = (f32[128]{0:T(128)}, f32[128]{0:T(128)S(1)}, u32[]{:S(2)}) copy-start(f32[128]{0:T(128)S(1)} %fusion.115) | copy-start | bytes 1540
  377.6 72.7 %copy-start.33 = (bf16[2,128,1024]{2,1,0:T(8,128)(2,1)S(1)}, bf16[2,128,1024]{2,1,0:T(8,128)(2,1)}, u32[]{:S(2)}) copy-start(bf16[2,128,1024]{2,1,0:T(8,128)(2,1)} %param.37) | copy-start | bytes 1572868
  529.3 178.7 %reduce-scatter.9.cloned.1.call-start = ((), (), s32[]{:S(2)}) async-start(), calls=%async_computation.13 | async-start | bytes 4718592 | tf_op jit(solution)/shard_map/reduce_scatter | solution.py:237
  578.2 276.5 %reduce-scatter.13.cloned.1.call-start = ((), (), s32[]{:S(2)}) async-start(), calls=%async_computation.15 | async-start | bytes 4325376 | tf_op jit(solution)/shard_map/reduce_scatter | solution.py:249
  582.8 431.8 %reduce-scatter.11.cloned.1.call-start = ((), (), s32[]{:S(2)}) async-start(), calls=%async_computation.14 | async-start | bytes 12976128 | tf_op jit(solution)/shard_map/reduce_scatter | solution.py:248
  584.2 123.9 %copy-start.59 = (f32[128]{0:T(128)S(1)}, f32[128]{0:T(128)}, u32[]{:S(2)}) copy-start(f32[128]{0:T(128)} %copy-done.58) | copy-start | bytes 1540
  584.2 123.8 %copy-start.68 = (f32[128]{0:T(128)S(1)}, f32[128]{0:T(128)}, u32[]{:S(2)}) copy-start(f32[128]{0:T(128)} %copy-done.67) | copy-start | bytes 1540
  719.3 655.5 %reduce-scatter.15.cloned.1.call-start = ((), (), s32[]{:S(2)}) async-start(), calls=%async_computation.16 | async-start | bytes 17301504 | tf_op jit(solution)/shard_map/reduce_scatter | solution.py:250
  732.3 1002.7 %reduce-scatter.17.cloned.1.call-start = ((), (), s32[]{:S(2)}) async-start(), calls=%async_computation.17 | async-start | bytes 17301504 | tf_op jit(solution)/shard_map/reduce_scatter | solution.py:251
  779.6 48.2 %copy-start.18 = (f32[128,1024]{1,0:T(8,128)S(1)}, f32[128,1024]{1,0:T(8,128)}, u32[]{:S(2)}) copy-start(f32[128,1024]{1,0:T(8,128)} %copy-done.17) | copy-start | bytes 1572868
  779.6 48.2 %copy-start.20 = (f32[128,1024]{1,0:T(8,128)S(1)}, f32[128,1024]{1,0:T(8,128)}, u32[]{:S(2)}) copy-start(f32[128,1024]{1,0:T(8,128)} %copy-done.19) | copy-start | bytes 1572868
  779.6 48.2 %copy-start.84 = (f32[128]{0:T(128)S(1)}, f32[128]{0:T(128)}, u32[]{:S(2)}) copy-start(f32[128]{0:T(128)} %copy-done.83) | copy-start | bytes 1540
  779.6 48.2 %copy-start.86 = (f32[128]{0:T(128)S(1)}, f32[128]{0:T(128)}, u32[]{:S(2)}) copy-start(f32[128]{0:T(128)} %copy-done.85) | copy-start | bytes 1540
  (82 other events, 720.9 us)
Sparse Core Ops, SparseCore 0:
  10.9 72.2 all-gather.6
  88.2 71.9 all-gather.16
  162.9 71.6 all-gather.8
  237.5 54.7 all-gather.10
  295.1 76.2 all-gather.12
  374.2 75.9 all-gather.14
  529.4 86.6 reduce-scatter.6
  620.2 87.8 reduce-scatter.8
  710.9 143.7 reduce-scatter.12
  861.1 153.4 reduce-scatter.10
  1017.6 357.1 reduce-scatter.14
  1377.6 357.3 reduce-scatter.16
where the time goes:
time: 1750 us; the launch traced here: 1740 us
  waiting for transfers between devices  1310 us (75%)
  matrix products  199 us (11%)
  blocking collectives  105 us (6%)
  local copies, waits for them, and re-layouts  82.9 us (5%)
  other arithmetic  29.3 us (2%)
    reduce_scatter x1, waiting for transfers between devices, body(): lax.psum_scatter(local_up, ('dp', 'fsdp'), scatter_dimension=0, tiled=True)  360 us
    reduce_scatter x1, waiting for transfers between devices, body(): lax.psum_scatter(local_down, ('dp', 'fsdp'), scatter_dimension=0, tiled=T...  360 us
    reduce_scatter x1, waiting for transfers between devices, body(): lax.psum_scatter(local_qkv, ('dp', 'fsdp'), scatter_dimension=0, tiled=True)  160 us
    reduce_scatter x2, waiting for transfers between devices, body(): lax.psum_scatter(grad_pairs.astype(jnp.bfloat16), 'fsdp', scatter_dimensi...  116 us
    all_gather x2, waiting for transfers between devices, body(): kv_all = lax.all_gather(projected[:, width:], 'fsdp', axis=0, tiled=True)  86.2 us
    unnamed x2, blocking collectives  85.3 us
    all_gather x1, waiting for transfers between devices, body(): lax.all_gather(w_up, ('dp', 'fsdp'), axis=0, tiled=True)  75.8 us
    all_gather x1, waiting for transfers between devices, body(): lax.all_gather(w_down, ('dp', 'fsdp'), axis=0, tiled=True)  69.9 us
  transfers between devices with their start and end apart: 12, of which 12 were waited for; matrix products, arithmetic and copies ran while one was open for 13% of the time, Pallas kernels for 0%

commit v1 on v0

--- a/solution.py
+++ b/solution.py
@@ -191,7 +191,24 @@
             jnp.bfloat16
         )
         query_cols = projected[:, :width]
-        kv_all = lax.all_gather(projected[:, width:], "fsdp", axis=0, tiled=True)
+        shard = projected[:, width:]
+        count, position, rows = (lax.axis_size("fsdp"), lax.axis_index("fsdp"), shard.shape[0])
+        route = [(i, (i + 1) % count) for i in range(count)]
+        backward = [(i, (i - 1) % count) for i in range(count)]
+        kv_all = jnp.zeros((*shard.shape[:0], count * rows, *shard.shape[0 + 1 :]), shard.dtype)
+        kv_all = lax.dynamic_update_slice_in_dim(kv_all, shard, position * rows, axis=0)
+        from_left = from_right = shard
+        halfway = count // 2
+        for step in range(1, halfway + 1):
+            from_left = lax.ppermute(from_left, "fsdp", route)
+            kv_all = lax.dynamic_update_slice_in_dim(
+                kv_all, from_left, (position - step) % count * rows, axis=0
+            )
+            if step < count - halfway:
+                from_right = lax.ppermute(from_right, "fsdp", backward)
+                kv_all = lax.dynamic_update_slice_in_dim(
+                    kv_all, from_right, (position + step) % count * rows, axis=0
+                )
         mixed_low, log_total = attention_forward(query_cols, kv_all, own_scene, key_scene)
         hidden = block_tokens + jnp.dot(mixed_low, full_out, preferred_element_type=jnp.float32)
         normed_two, pull_two = jax.vjp(

time: 1750 us -> 1670 us (0.954)
  waiting for transfers between devices: 1310 us -> 1170 us
  local copies, waits for them, and re-layouts: 82.9 us -> 105 us
  starting transfers between devices: 0.86 us -> 21.1 us
  blocking collectives: 105 us -> 123 us
    ppermute x0 -> x14, waiting for transfers between devices: none -> 117 us  [the longest x6 97.6 us: body(): from_right = lax.ppermute(from_right, 'fsdp', backward)]
    all_gather x2 -> x0, waiting for transfers between devices: 86.2 us -> none  [body(): kv_all = lax.all_gather(projected[:, width:], 'fsdp', axis=0, tiled=True)]
    all_gather x1, waiting for transfers between devices: 75.8 us -> 0.02 us  [body(): lax.all_gather(w_up, ('dp', 'fsdp'), axis=0, tiled=True)]
    all_gather x1, waiting for transfers between devices: 69.9 us -> 5.15 us  [body(): lax.all_gather(w_down, ('dp', 'fsdp'), axis=0, tiled=True)]
    all_gather x1, waiting for transfers between devices: 24.1 us -> 0.02 us  [body(): lax.all_gather(w_out, ('dp', 'fsdp'), axis=0, tiled=True)]
    all_gather x1, blocking collectives: 19.6 us -> 39.9 us  [body(): all_scenes = lax.all_gather(scene_ids, 'fsdp', axis=2, tiled=True)]
    ppermute x0 -> x14, starting transfers between devices: none -> 20.1 us  [the longest x8 11.2 us: body(): from_left = lax.ppermute(from_left, 'fsdp', route)]
    dynamic_update_slice x0 -> x14, local copies, waits for them, and re-layouts: none -> 18.1 us  [the longest x8 11 us: body(): lax.dynamic_update_slice_in_dim(kv_all, from_left, (position - step) % co...]
  transfers between devices with their start and end apart: 12 -> 24, of which waited for: 12 -> 14; matrix products, arithmetic and copies ran while one was open for 13% -> 15% of each run, Pallas kernels for 0% -> 0%
where the time goes in v1:
time: 1670 us
  waiting for transfers between devices  1170 us (70%)
  matrix products  197 us (12%)
  blocking collectives  123 us (7%)
  local copies, waits for them, and re-layouts  105 us (6%)
  other arithmetic  29.3 us (2%)
  starting transfers between devices  21.1 us (1%)
    reduce_scatter x1, waiting for transfers between devices, body(): lax.psum_scatter(local_up, ('dp', 'fsdp'), scatter_dimension=0, tiled=True)  360 us
    reduce_scatter x1, waiting for transfers between devices, body(): lax.psum_scatter(local_down, ('dp', 'fsdp'), scatter_dimension=0, tiled=T...  360 us
    reduce_scatter x1, waiting for transfers between devices, body(): lax.psum_scatter(local_qkv, ('dp', 'fsdp'), scatter_dimension=0, tiled=True)  160 us
    reduce_scatter x2, waiting for transfers between devices, body(): lax.psum_scatter(grad_pairs.astype(jnp.bfloat16), 'fsdp', scatter_dimensi...  116 us
    ppermute x6, waiting for transfers between devices, body(): from_right = lax.ppermute(from_right, 'fsdp', backward)  97.6 us
    unnamed x2, blocking collectives  83.6 us
    dot_general x8, matrix products, outer_sum(): jnp.einsum('ti,tj->ij', left, right, preferred_element_type=jnp.float32)  58.6 us
    all_gather x1, blocking collectives, body(): all_scenes = lax.all_gather(scene_ids, 'fsdp', axis=2, tiled=True)  39.9 us
  transfers between devices with their start and end apart: 24, of which 14 were waited for; matrix products, arithmetic and copies ran while one was open for 15% of the time, Pallas kernels for 0%

profile of v1, /device:TPU:0, one launch (start us, length us, event | category | flops | bytes accessed | tf_op | source)
XLA Modules:
  0.0 1665.8 jit_solution(3837942153092849710)
XLA Ops:
  12.8 42.3 %all-reduce.9 = (bf16[1024]{0:T(1024)(128)(2,1)S(1)}, bf16[1024]{0:T(1024)(128)(2,1)S(1)}, bf16[1024]{0:T(1024)(128)(2,1)S(1)}, bf16[1024]{0:T(1024)(128)(2,1)S(1)}) all-reduce(bf16[1024]{0:T(1024)(128)(2,1)S(1)} %dynamic-update-slice.1, bf16[1024]{0:T(1024)(128)(2,1)S(1)} %dynamic-update-slice, ...), channel_id=1, replica_groups=mesh['dp'=4,'fsdp'=8] {'dp','fsdp'}, use_global_device_ids=true, to_apply=%add.1 | all-reduce | flops 4096 | bytes 16384
  58.3 25.1 %all-gather.5.cloned.1.call-done = bf16[1024,3072]{1,0:T(8,128)(2,1)} async-done(((bf16[32,3072]{1,0:T(8,128)(2,1)}), bf16[1024,3072]{1,0:T(8,128)(2,1)}) %all-gather.5.cloned.1.call-update) | async-done | bytes 6291472 | tf_op jit(solution)/shard_map/all_gather | solution.py:170
  98.5 39.9 %all_gather.21 = s32[2,1,1024]{2,1,0:T(1,128)S(1)} all-gather(s32[2,1,128]{2,1,0:T(1,128)S(1)} %copy-done.84), channel_id=1, replica_groups=mesh['dp'=4,'fsdp'=8] {'fsdp'}, dimensions={2}, use_global_device_ids=true | all-gather | bytes 9216 | tf_op jit(solution)/shard_map/all_gather | solution.py:155
  149.2 30.5 %collective-permute-done.1 = bf16[128,2048]{1,0:T(8,128)(2,1)} collective-permute-done((bf16[128,2048]{1,0:T(8,128)(2,1)}, bf16[128,2048]{1,0:T(8,128)(2,1)}, u32[]{:S(2)}, u32[]{:S(2)}) %collective-permute-start.1) | collective-permute-done | bytes 524320 | tf_op jit(solution)/shard_map/ppermute | solution.py:208
  185.5 18.4 %collective-permute-done.10 = bf16[128,2048]{1,0:T(8,128)(2,1)S(1)} collective-permute-done((bf16[128,2048]{1,0:T(8,128)(2,1)}, bf16[128,2048]{1,0:T(8,128)(2,1)S(1)}, u32[]{:S(2)}, u32[]{:S(2)}) %collective-permute-start.10) | collective-permute-done | bytes 524320 | tf_op jit(solution)/shard_map/ppermute | solution.py:208
  208.6 21.6 %collective-permute-done.3 = bf16[128,2048]{1,0:T(8,128)(2,1)S(1)} collective-permute-done((bf16[128,2048]{1,0:T(8,128)(2,1)}, bf16[128,2048]{1,0:T(8,128)(2,1)S(1)}, u32[]{:S(2)}, u32[]{:S(2)}) %collective-permute-start.3) | collective-permute-done | bytes 524320 | tf_op jit(solution)/shard_map/ppermute | solution.py:208
  233.9 19.0 %collective-permute-done.4 = bf16[128,2048]{1,0:T(8,128)(2,1)} collective-permute-done((bf16[128,2048]{1,0:T(8,128)(2,1)S(1)}, bf16[128,2048]{1,0:T(8,128)(2,1)}, u32[]{:S(2)}, u32[]{:S(2)}) %collective-permute-start.4) | collective-permute-done | bytes 524320 | tf_op jit(solution)/shard_map/ppermute | solution.py:203
  259.2 27.0 %collective-permute-done.5 = bf16[128,2048]{1,0:T(8,128)(2,1)S(1)} collective-permute-done((bf16[128,2048]{1,0:T(8,128)(2,1)S(1)}, bf16[128,2048]{1,0:T(8,128)(2,1)S(1)}, u32[]{:S(2)}, u32[]{:S(2)}) %collective-permute-start.5) | collective-permute-done | bytes 524320 | tf_op jit(solution)/shard_map/ppermute | solution.py:208
  294.1 16.0 while.98
  310.1 10.1 while.99
  329.7 16.1 while.96
  345.7 10.3 while.97
  374.8 10.1 add_convert_fusion
  391.8 7.8 add_convert_fusion.1
  408.0 8.9 while.100
  419.4 34.4 %while.101 = (s32[]{:T(128)}, f32[128,16,64]{0,2,1:T(8,128)}, bf16[2,512,2048]{2,1,0:T(8,128)(2,1)}, bf16[2,512,2048]{1,2,0:T(8,128)(2,1)}, s32[1,1,128]{2,1,0:T...) while((s32[]{:T(128)}, f32[128,16,64]{0,2,1:T(8,128)}, ...), condition=%wide.region_26.27_spmd.clone, body=%wide.region_25.26_spmd.clone.sunk | while | flops 687276032 | bytes 83065600 | solution.py:137
  454.8 10.9 while.102
  468.3 34.3 %while.103 = (s32[]{:T(128)}, f32[128,16,64]{0,2,1:T(8,128)}, bf16[2,512,2048]{2,1,0:T(8,128)(2,1)}, bf16[2,512,2048]{1,2,0:T(8,128)(2,1)}, s32[1,1,128]{2,1,0:T...) while((s32[]{:T(128)}, f32[128,16,64]{0,2,1:T(8,128)}, ...), condition=%wide.region_36.37_spmd.clone, body=%wide.region_35.36_spmd.clone.sunk | while | flops 687276032 | bytes 80968392 | solution.py:137
  508.6 32.0 %reduce-scatter.7.cloned.1.call-done = bf16[128,2048]{1,0:T(8,128)(2,1)} async-done(((bf16[1024,2048]{1,0:T(8,128)(2,1)}), bf16[128,2048]{1,0:T(8,128)(2,1)}) %reduce-scatter.7.cloned.1.call-update) | async-done | bytes 524304 | tf_op jit(solution)/shard_map/reduce_scatter | solution.py:254
  540.6 7.5 fusion.95
  548.1 84.1 %reduce-scatter.9.cloned.1.call-done = bf16[128,2048]{1,0:T(8,128)(2,1)} async-done(((bf16[1024,2048]{1,0:T(8,128)(2,1)}), bf16[128,2048]{1,0:T(8,128)(2,1)}) %reduce-scatter.9.cloned.1.call-update) | async-done | bytes 524304 | tf_op jit(solution)/shard_map/reduce_scatter | solution.py:254
  632.2 11.2 convolution_add_fusion.2
  648.2 8.3 convolution_add_fusion.1
  657.5 11.2 fusion.104
  668.7 13.3 convolution_add_fusion
  682.8 9.6 fusion.68
  692.4 8.2 fusion.69
  706.8 41.3 %all-reduce.8 = (f32[1024]{0:T(1024)S(1)}, f32[1024]{0:T(1024)S(1)}, f32[1024]{0:T(1024)S(1)}, f32[1024]{0:T(1024)S(1)}) all-reduce(f32[1024]{0:T(1024)S(1)} %add.333, f32[1024]{0:T(1024)S(1)} %add.334, f32[1024]{0:T(1024)S(1)} %add.335, f32[1024]{0:T(1024)S(1)} %add.336), channel_id=16, replica_groups=mesh['dp'=4,'fsdp'=8] {'dp','fsdp'}, use_global_device_ids=true, to_apply=%region_49.50.clone | all-reduce | flops 4096 | bytes 32768
  751.9 26.8 %reduce-scatter.13.cloned.1.call-done = f32[32,1024]{1,0:T(8,128)} async-done(((f32[1024,1024]{1,0:T(8,128)}), f32[32,1024]{1,0:T(8,128)}) %reduce-scatter.13.cloned.1.call-update) | async-done | bytes 131088 | tf_op jit(solution)/shard_map/reduce_scatter | solution.py:266
  778.8 159.6 %reduce-scatter.11.cloned.1.call-done = f32[32,3072]{1,0:T(8,128)} async-done(((f32[1024,3072]{1,0:T(8,128)}), f32[32,3072]{1,0:T(8,128)}) %reduce-scatter.11.cloned.1.call-update) | async-done | bytes 393232 | tf_op jit(solution)/shard_map/reduce_scatter | solution.py:265
  938.4 360.2 %reduce-scatter.15.cloned.1.call-done = f32[32,4096]{1,0:T(8,128)} async-done(((f32[1024,4096]{1,0:T(8,128)}), f32[32,4096]{1,0:T(8,128)}) %reduce-scatter.15.cloned.1.call-update) | async-done | bytes 524304 | tf_op jit(solution)/shard_map/reduce_scatter | solution.py:267
  1298.6 360.2 %reduce-scatter.17.cloned.1.call-done = f32[128,1024]{1,0:T(8,128)} async-done(((f32[4096,1024]{1,0:T(8,128)}), f32[128,1024]{1,0:T(8,128)}) %reduce-scatter.17.cloned.1.call-update) | async-done | bytes 524304 | tf_op jit(solution)/shard_map/reduce_scatter | solution.py:268
  (498 shorter events, 273.3 us)
Async XLA Ops:
  7.2 76.1 %all-gather.5.cloned.1.call-start = ((), (), s32[]{:S(2)}) async-start(), calls=%async_computation.6 | async-start | bytes 6488064 | tf_op jit(solution)/shard_map/all_gather | solution.py:170
  7.9 349.2 %all-gather.7.cloned.1.call-start = ((), (), s32[]{:S(2)}) async-start(), calls=%async_computation.7 | async-start | bytes 2162688 | tf_op jit(solution)/shard_map/all_gather | solution.py:171
  8.7 351.9 %all-gather.9.cloned.1.call-start = ((), (), s32[]{:S(2)}) async-start(), calls=%async_computation.8 | async-start | bytes 8650752 | tf_op jit(solution)/shard_map/all_gather | solution.py:172
  9.4 365.4 %all-gather.11.cloned.1.call-start = ((), (), s32[]{:S(2)}) async-start(), calls=%async_computation.9 | async-start | bytes 8650752 | tf_op jit(solution)/shard_map/all_gather | solution.py:173
  88.9 51.7 %collective-permute-start.7 = (bf16[128,2048]{1,0:T(8,128)(2,1)}, bf16[128,2048]{1,0:T(8,128)(2,1)}, u32[]{:S(2)}, u32[]{:S(2)}) collective-permute-start(bf16[128,2048]{1,0:T(8,128)(2,1)} %get-tuple-element.1002), channel_id=1, source_target_pairs={{0,1},{1,2},{2,3},{3,4},{4,5},{5,6},{6,7},{7,0},{8,9},{9,10},{10,1... | collective-permute-start | bytes 1572872 | tf_op jit(solution)/shard_map/ppermute | solution.py:203
  90.4 50.8 %collective-permute-start.8 = (bf16[128,2048]{1,0:T(8,128)(2,1)}, bf16[128,2048]{1,0:T(8,128)(2,1)}, u32[]{:S(2)}, u32[]{:S(2)}) collective-permute-start(bf16[128,2048]{1,0:T(8,128)(2,1)} %get-tuple-element.1002), channel_id=1, source_target_pairs={{0,7},{1,0},{2,1},{3,2},{4,3},{5,4},{6,5},{7,6},{8,15},{9,8},{10,9... | collective-permute-start | bytes 1572872 | tf_op jit(solution)/shard_map/ppermute | solution.py:208
  98.4 47.0 %collective-permute-start = (bf16[128,2048]{1,0:T(8,128)(2,1)}, bf16[128,2048]{1,0:T(8,128)(2,1)}, u32[]{:S(2)}, u32[]{:S(2)}) collective-permute-start(bf16[128,2048]{1,0:T(8,128)(2,1)} %get-tuple-element.1000), channel_id=1, source_target_pairs={{0,1},{1,2},{2,3},{3,4},{4,5},{5,6},{6,7},{7,0},{8,9},{9,10},{10,1... | collective-permute-start | bytes 1572872 | tf_op jit(solution)/shard_map/ppermute | solution.py:203
  98.4 442.2 %reduce-scatter.7.cloned.1.call-start = ((), (), s32[]{:S(2)}) async-start(), calls=%async_computation.10 | async-start | bytes 4718592 | tf_op jit(solution)/shard_map/reduce_scatter | solution.py:254
  138.4 41.3 %collective-permute-start.1 = (bf16[128,2048]{1,0:T(8,128)(2,1)}, bf16[128,2048]{1,0:T(8,128)(2,1)}, u32[]{:S(2)}, u32[]{:S(2)}) collective-permute-start(bf16[128,2048]{1,0:T(8,128)(2,1)} %get-tuple-element.1000), channel_id=1, source_target_pairs={{0,7},{1,0},{2,1},{3,2},{4,3},{5,4},{6,5},{7,6},{8,15},{9,8},{10,9... | collective-permute-start | bytes 1572872 | tf_op jit(solution)/shard_map/ppermute | solution.py:208
  140.1 226.8 %copy-start.47 = (f32[1024]{0:T(1024)}, f32[1024]{0:T(1024)S(1)}, u32[]{:S(2)}) copy-start(f32[1024]{0:T(1024)S(1)} %convert_element_type.139) | copy-start | bytes 12292
  140.1 263.1 %copy-start.43 = (f32[1024]{0:T(1024)}, f32[1024]{0:T(1024)S(1)}, u32[]{:S(2)}) copy-start(f32[1024]{0:T(1024)S(1)} %convert_element_type.138) | copy-start | bytes 12292
  140.6 42.9 %collective-permute-start.9 = (bf16[128,2048]{1,0:T(8,128)(2,1)}, bf16[128,2048]{1,0:T(8,128)(2,1)S(1)}, u32[]{:S(2)}, u32[]{:S(2)}) collective-permute-start(bf16[128,2048]{1,0:T(8,128)(2,1)} %collective-permute-done.7), channel_id=1, source_target_pairs={{0,1},{1,2},{2,3},{3,4},{4,5},{5,6},{6,7},{7,0},{8,9},{9,10},{10,1... | collective-permute-start | bytes 1572872 | tf_op jit(solution)/shard_map/ppermute | solution.py:203
  141.2 62.7 %collective-permute-start.10 = (bf16[128,2048]{1,0:T(8,128)(2,1)}, bf16[128,2048]{1,0:T(8,128)(2,1)S(1)}, u32[]{:S(2)}, u32[]{:S(2)}) collective-permute-start(bf16[128,2048]{1,0:T(8,128)(2,1)} %collective-permute-done.8), channel_id=1, source_target_pairs={{0,7},{1,0},{2,1},{3,2},{4,3},{5,4},{6,5},{7,6},{8,15},{9,8},{10,9... | collective-permute-start | bytes 1572872 | tf_op jit(solution)/shard_map/ppermute | solution.py:208
  145.4 59.2 %collective-permute-start.2 = (bf16[128,2048]{1,0:T(8,128)(2,1)}, bf16[128,2048]{1,0:T(8,128)(2,1)S(1)}, u32[]{:S(2)}, u32[]{:S(2)}) collective-permute-start(bf16[128,2048]{1,0:T(8,128)(2,1)} %collective-permute-done), channel_id=1, source_target_pairs={{0,1},{1,2},{2,3},{3,4},{4,5},{5,6},{6,7},{7,0},{8,9},{9,10},{10,1... | collective-permute-start | bytes 1572872 | tf_op jit(solution)/shard_map/ppermute | solution.py:203
  179.7 50.5 %collective-permute-start.3 = (bf16[128,2048]{1,0:T(8,128)(2,1)}, bf16[128,2048]{1,0:T(8,128)(2,1)S(1)}, u32[]{:S(2)}, u32[]{:S(2)}) collective-permute-start(bf16[128,2048]{1,0:T(8,128)(2,1)} %collective-permute-done.1), channel_id=1, source_target_pairs={{0,7},{1,0},{2,1},{3,2},{4,3},{5,4},{6,5},{7,6},{8,15},{9,8},{10,9... | collective-permute-start | bytes 1572872 | tf_op jit(solution)/shard_map/ppermute | solution.py:208
  183.5 48.4 %collective-permute-start.11 = (bf16[128,2048]{1,0:T(8,128)(2,1)S(1)}, bf16[128,2048]{1,0:T(8,128)(2,1)S(1)}, u32[]{:S(2)}, u32[]{:S(2)}) collective-permute-start(bf16[128,2048]{1,0:T(8,128)(2,1)S(1)} %collective-permute-done.9), channel_id=1, source_target_pairs={{0,1},{1,2},{2,3},{3,4},{4,5},{5,6},{6,7},{7,0},{8,9},{9,10},{10,1... | collective-permute-start | bytes 1572872 | tf_op jit(solution)/shard_map/ppermute | solution.py:203
  204.0 54.4 %collective-permute-start.12 = (bf16[128,2048]{1,0:T(8,128)(2,1)S(1)}, bf16[128,2048]{1,0:T(8,128)(2,1)S(1)}, u32[]{:S(2)}, u32[]{:S(2)}) collective-permute-start(bf16[128,2048]{1,0:T(8,128)(2,1)S(1)} %collective-permute-done.10), channel_id=1, source_target_pairs={{0,7},{1,0},{2,1},{3,2},{4,3},{5,4},{6,5},{7,6},{8,15},{9,8},{10,9... | collective-permute-start | bytes 1572872 | tf_op jit(solution)/shard_map/ppermute | solution.py:208
  204.6 48.3 %collective-permute-start.4 = (bf16[128,2048]{1,0:T(8,128)(2,1)S(1)}, bf16[128,2048]{1,0:T(8,128)(2,1)}, u32[]{:S(2)}, u32[]{:S(2)}) collective-permute-start(bf16[128,2048]{1,0:T(8,128)(2,1)S(1)} %collective-permute-done.2), channel_id=1, source_target_pairs={{0,1},{1,2},{2,3},{3,4},{4,5},{5,6},{6,7},{7,0},{8,9},{9,10},{10,1... | collective-permute-start | bytes 1572872 | tf_op jit(solution)/shard_map/ppermute | solution.py:203
  230.2 56.0 %collective-permute-start.5 = (bf16[128,2048]{1,0:T(8,128)(2,1)S(1)}, bf16[128,2048]{1,0:T(8,128)(2,1)S(1)}, u32[]{:S(2)}, u32[]{:S(2)}) collective-permute-start(bf16[128,2048]{1,0:T(8,128)(2,1)S(1)} %collective-permute-done.3), channel_id=1, source_target_pairs={{0,7},{1,0},{2,1},{3,2},{4,3},{5,4},{6,5},{7,6},{8,15},{9,8},{10,9... | collective-permute-start | bytes 1572872 | tf_op jit(solution)/shard_map/ppermute | solution.py:208
  231.9 55.1 %collective-permute-start.13 = (bf16[128,2048]{1,0:T(8,128)(2,1)S(1)}, bf16[128,2048]{1,0:T(8,128)(2,1)S(1)}, u32[]{:S(2)}, u32[]{:S(2)}) collective-permute-start(bf16[128,2048]{1,0:T(8,128)(2,1)S(1)} %collective-permute-done.11), channel_id=1, source_target_pairs={{0,1},{1,2},{2,3},{3,4},{4,5},{5,6},{6,7},{7,0},{8,9},{9,10},{10,1... | collective-permute-start | bytes 1572872 | tf_op jit(solution)/shard_map/ppermute | solution.py:203
  252.9 68.5 %collective-permute-start.6 = (bf16[128,2048]{1,0:T(8,128)(2,1)}, bf16[128,2048]{1,0:T(8,128)(2,1)}, u32[]{:S(2)}, u32[]{:S(2)}) collective-permute-start(bf16[128,2048]{1,0:T(8,128)(2,1)} %collective-permute-done.4), channel_id=1, source_target_pairs={{0,1},{1,2},{2,3},{3,4},{4,5},{5,6},{6,7},{7,0},{8,9},{9,10},{10,1... | collective-permute-start | bytes 1572872 | tf_op jit(solution)/shard_map/ppermute | solution.py:203
  453.9 178.3 %reduce-scatter.9.cloned.1.call-start = ((), (), s32[]{:S(2)}) async-start(), calls=%async_computation.11 | async-start | bytes 4718592 | tf_op jit(solution)/shard_map/reduce_scatter | solution.py:254
  502.6 276.1 %reduce-scatter.13.cloned.1.call-start = ((), (), s32[]{:S(2)}) async-start(), calls=%async_computation.13 | async-start | bytes 4325376 | tf_op jit(solution)/shard_map/reduce_scatter | solution.py:266
  507.2 431.2 %reduce-scatter.11.cloned.1.call-start = ((), (), s32[]{:S(2)}) async-start(), calls=%async_computation.12 | async-start | bytes 12976128 | tf_op jit(solution)/shard_map/reduce_scatter | solution.py:265
  508.6 123.6 %copy-start.61 = (f32[128]{0:T(128)S(1)}, f32[128]{0:T(128)}, u32[]{:S(2)}) copy-start(f32[128]{0:T(128)} %copy-done.60) | copy-start | bytes 1540
  508.6 123.6 %copy-start.70 = (f32[128]{0:T(128)S(1)}, f32[128]{0:T(128)}, u32[]{:S(2)}) copy-start(f32[128]{0:T(128)} %copy-done.69) | copy-start | bytes 1540
  643.5 655.1 %reduce-scatter.15.cloned.1.call-start = ((), (), s32[]{:S(2)}) async-start(), calls=%async_computation.14 | async-start | bytes 17301504 | tf_op jit(solution)/shard_map/reduce_scatter | solution.py:267
  656.5 1002.3 %reduce-scatter.17.cloned.1.call-start = ((), (), s32[]{:S(2)}) async-start(), calls=%async_computation.15 | async-start | bytes 17301504 | tf_op jit(solution)/shard_map/reduce_scatter | solution.py:268
  703.8 46.6 %copy-start.20 = (f32[128,1024]{1,0:T(8,128)S(1)}, f32[128,1024]{1,0:T(8,128)}, u32[]{:S(2)}) copy-start(f32[128,1024]{1,0:T(8,128)} %copy-done.19) | copy-start | bytes 1572868
  703.8 46.6 %copy-start.22 = (f32[128,1024]{1,0:T(8,128)S(1)}, f32[128,1024]{1,0:T(8,128)}, u32[]{:S(2)}) copy-start(f32[128,1024]{1,0:T(8,128)} %copy-done.21) | copy-start | bytes 1572868
  703.8 46.6 %copy-start.86 = (f32[128]{0:T(128)S(1)}, f32[128]{0:T(128)}, u32[]{:S(2)}) copy-start(f32[128]{0:T(128)} %copy-done.85) | copy-start | bytes 1540
  703.8 46.6 %copy-start.88 = (f32[128]{0:T(128)S(1)}, f32[128]{0:T(128)}, u32[]{:S(2)}) copy-start(f32[128]{0:T(128)} %copy-done.87) | copy-start | bytes 1540
  (96 other events, 1038.1 us)
Sparse Core Ops, SparseCore 0:
  10.9 72.3 all-gather.4
  86.3 93.3 all-gather.6
  182.7 113.1 all-gather.8
  298.7 76.0 all-gather.10
  454.0 86.5 reduce-scatter.6
  544.5 87.6 reduce-scatter.8
  635.0 143.7 reduce-scatter.12
  785.4 152.9 reduce-scatter.10
  941.4 357.1 reduce-scatter.14
  1301.4 357.3 reduce-scatter.16
